TPU v7x, 32 devices: a whole 2x2x4 slice. The times are simulated.
32 devices in a mesh: groups: 2 (over x), level: 16 (over z, y, core).
Axes of the slice: x: 2, y: 2, z: 4, core: 2. Of those that a mesh axis runs over, the one named last changes fastest.
Arguments:
- latents: bfloat16 [64, 256, 640], P(('groups', 'level')), parts along dimension 0, may hold values from -6 to 6
- levels: int32 [64], P(('groups', 'level')), parts along dimension 0, may hold values from 0 to 15
- back_reach: int32 [64], P(('groups', 'level')), parts along dimension 0, may hold values from 1 to 2
- text_ids: int32 [154], P('groups'), parts along dimension 0, may hold values from 0 to 49407
- text_table: bfloat16 [49408, 1024], P('level'), may hold values from -6 to 6
- text_proj: bfloat16 [1024, 640], replicated, may hold values from -0.75 to 0.75
- level_embed: float32 [16, 640], replicated, may hold values from -3 to 3
- step_rate: float32 [16], replicated, may hold values from 0.3 to 1
- norm_gain: float32 [640], replicated, may hold values from 0.5 to 1.5
- w_query: bfloat16 [640, 640], replicated
- w_key: bfloat16 [640, 640], replicated
- w_value: bfloat16 [640, 640], replicated, may hold values from -0.25 to 0.25
- w_out: bfloat16 [640, 640], replicated, may hold values from -0.25 to 0.25
Outputs:
- queue_out: bfloat16 [64, 256, 640], P(('groups', 'level')), parts along dimension 0
There are 2 independent parts, one for each index of `groups`. A program takes and returns all parts, laid end to end along the dimension named above; an argument that names none is the same for every part. Nothing has to cross between parts.
All inputs are finite; a program needn't handle non-finite values.
Results may differ from a plain program's by a relative error of at most 0.007.
Values may be sent and summed in bfloat16 or wider, within the bound.
A program may use at most 64 MiB of HBM per device.

v0:
```python
import jax
import jax.numpy as jnp
from jax import lax
from jax.sharding import PartitionSpec as P

DH = 64
BAND = 2
STEPS = 3


def extended(block, sides, width):
    for axis, dim in sides:
        count = lax.axis_size(axis)
        forward = [(i, i + 1) for i in range(count - 1)]
        forward.append((count - 1, 0))
        backward = [(target, source) for source, target in forward]
        low = lax.ppermute(
            lax.slice_in_dim(block, block.shape[dim] - width, None, axis=dim), axis, forward
        )
        high = lax.ppermute(lax.slice_in_dim(block, 0, width, axis=dim), axis, backward)
        block = jnp.concatenate([low, block, high], axis=dim)
    return block


def shifted_2(block, axis, distance):
    devices = range(lax.axis_size(axis))
    route = [((i - distance) % len(devices), i) for i in devices]
    return lax.ppermute(block, axis, route)


def per_device(
    latents,
    levels,
    back_reach,
    text_ids,
    text_table,
    text_proj,
    level_embed,
    step_rate,
    norm_gain,
    w_query,
    w_key,
    w_value,
    w_out,
):
    count = lax.axis_size("level")
    index = lax.axis_index("level")
    frames_dev, tokens, width = latents.shape
    heads = width // DH
    scale = 1.0 / DH**0.5
    total_frames = frames_dev * count
    vocab_rows = text_table.shape[0]
    one_text = (
        text_ids[:, None] == index * vocab_rows + jnp.arange(vocab_rows, dtype=jnp.int32)[None, :]
    ).astype(jnp.bfloat16)
    text_local = jnp.dot(one_text, text_table, preferred_element_type=jnp.float32)
    pooled = jnp.mean(lax.psum(text_local, "level"), axis=0)
    text_vec = jnp.dot(
        pooled.astype(jnp.bfloat16)[None, :], text_proj, preferred_element_type=jnp.float32
    )[0]
    level_count = level_embed.shape[0]

    def project(source, weight):
        flat = source.reshape(-1, width)
        return (
            jnp.dot(flat, weight, preferred_element_type=jnp.float32)
            .astype(jnp.bfloat16)
            .reshape(source.shape[0], tokens, heads, DH)
        )

    current = latents
    for step in range(STEPS):
        one_level = (levels[:, None] == jnp.arange(level_count, dtype=jnp.int32)[None, :]).astype(
            jnp.float32
        )
        cond = jnp.dot(one_level, level_embed, precision=lax.Precision.HIGHEST) + text_vec[None, :]
        rate = jnp.dot(one_level, step_rate[:, None], precision=lax.Precision.HIGHEST)[:, 0]
        hin = current.astype(jnp.float32) + cond[:, None, :]
        normed = (
            hin * lax.rsqrt(jnp.mean(hin * hin, axis=-1, keepdims=True) + 1e-06) * norm_gain
        ).astype(jnp.bfloat16)
        query = project(normed, w_query)
        paired = jnp.stack([project(normed, w_key), project(normed, w_value)])
        widened = extended(paired, (("level", 1),), BAND)
        keys = widened[0]
        values = widened[1]
        position = index * frames_dev + jnp.arange(frames_dev, dtype=jnp.int32)
        score_list = []
        valid_list = []
        for offset in range(-BAND, BAND + 1):
            shifted = keys[BAND + offset : BAND + offset + frames_dev]
            raw = (
                jnp.einsum("fphd,fphd->fph", query, shifted, preferred_element_type=jnp.float32)
                * scale
            )
            valid = (
                (offset >= -back_reach)
                & (position + offset >= 0)
                & (position + offset < total_frames)
            )
            score_list.append(jnp.where(valid[:, None, None], raw, -1e30))
            valid_list.append(valid.astype(jnp.float32)[:, None, None])
        scores = jnp.stack(score_list)
        masks = jnp.stack(valid_list)
        top = jnp.max(scores, axis=0)
        expo = jnp.exp(scores - top[None]) * masks
        weights = (expo / jnp.sum(expo, axis=0)[None]).astype(jnp.bfloat16)
        attended = jnp.zeros((frames_dev, tokens, heads, DH), jnp.float32)
        for slot, offset in enumerate(range(-BAND, BAND + 1)):
            shifted = values[BAND + offset : BAND + offset + frames_dev]
            attended = attended + weights[slot].astype(jnp.float32)[..., None] * shifted.astype(
                jnp.float32
            )
        attended = attended.astype(jnp.bfloat16).reshape(-1, width)
        noise_pred = jnp.dot(attended, w_out, preferred_element_type=jnp.float32).reshape(
            frames_dev, tokens, width
        )
        current = (current.astype(jnp.float32) - rate[:, None, None] * noise_pred).astype(
            jnp.bfloat16
        )
        current = shifted_2(current, "level", 1)
    return current


def solution(mesh):
    in_specs = (
        P(("groups", "level"), None, None),
        P(("groups", "level")),
        P(("groups", "level")),
        P("groups"),
        P("level", None),
        P(),
        P(),
        P(),
        P(),
        P(),
        P(),
        P(),
        P(),
    )
    out_specs = P(("groups", "level"), None, None)
    return jax.shard_map(
        per_device, mesh=mesh, in_specs=in_specs, out_specs=out_specs, check_vma=False
    )
```

profile of v0, /device:TPU:1, one launch (start us, length us, event | category | flops | bytes accessed | tf_op | source)
XLA Modules:
  0.0 281.0 jit_solution(11633380892146557952)
XLA Ops:
  6.5 4.9 %fusion.33 = f32[77,1024]{1,0:T(8,128)} fusion(bf16[3088,1024]{1,0:T(8,128)(2,1)} %param.17, s32[3088]{0:T(1024)S(1)} %iota_add_fusion, s32[77]{0:T(128)} %param.16), kind=kOutput, calls=%fused_computation.84 | convolution fusion | flops 487203008 | bytes 6652276 | tf_op jit(solution)/shard_map/dot_general | solution.py:56
  11.5 92.1 %all-reduce.2.cloned.1.call-done = f32[77,1024]{1,0:T(8,128)} async-done(((f32[77,1024]{1,0:T(8,128)}), f32[77,1024]{1,0:T(8,128)}) %all-reduce.2.cloned.1.call-update) | async-done | bytes 315408 | tf_op jit(solution)/shard_map/psum | solution.py:57
  114.0 2.1 convolution_convert_fusion.8
  117.2 2.0 reshape.375
  120.8 2.4 copy.96
  123.2 2.0 multiply_reduce_fusion.12
  125.2 15.7 %collective-permute-done = bf16[2,2,256,10,64]{2,4,3,1,0:T(8,128)(2,1)S(1)} collective-permute-done((bf16[2,2,256,10,64]{2,4,3,1,0:T(8,128)(2,1)}, bf16[2,2,256,10,64]{2,4,3,1,0:T(8,128)(2,1)S(1)}, u32[]{:S(2)}, u32[]{:S(2)}) %collective-permute-start) | collective-permute-done | bytes 1310752 | tf_op jit(solution)/shard_map/ppermute | solution.py:17
  140.9 9.5 %collective-permute-done.1 = bf16[2,2,256,10,64]{2,4,3,1,0:T(8,128)(2,1)S(1)} collective-permute-done((bf16[2,2,256,10,64]{2,4,3,1,0:T(8,128)(2,1)}, bf16[2,2,256,10,64]{2,4,3,1,0:T(8,128)(2,1)S(1)}, u32[]{:S(2)}, u32[]{:S(2)}) %collective-permute-start.1) | collective-permute-done | bytes 1310752 | tf_op jit(solution)/shard_map/ppermute | solution.py:20
  156.9 7.5 %collective-permute-done.2 = bf16[2,256,640]{2,1,0:T(8,128)(2,1)S(1)} collective-permute-done((bf16[2,256,640]{2,1,0:T(8,128)(2,1)S(1)}, bf16[2,256,640]{2,1,0:T(8,128)(2,1)S(1)}, u32[]{:S(2)}, u32[]{:S(2)}) %collective-permute-start.2) | collective-permute-done | bytes 655392 | tf_op jit(solution)/shard_map/ppermute | solution.py:28
  169.9 2.5 collective-permute-start.3
  173.4 2.1 convolution_convert_fusion.5
  176.6 2.0 reshape.377
  180.2 2.4 copy.104
  182.6 2.0 multiply_reduce_fusion.7
  184.6 16.7 %collective-permute-done.3 = bf16[2,2,256,10,64]{2,4,3,1,0:T(8,128)(2,1)S(1)} collective-permute-done((bf16[2,2,256,10,64]{2,4,3,1,0:T(8,128)(2,1)}, bf16[2,2,256,10,64]{2,4,3,1,0:T(8,128)(2,1)S(1)}, u32[]{:S(2)}, u32[]{:S(2)}) %collective-permute-start.3) | collective-permute-done | bytes 1310752 | tf_op jit(solution)/shard_map/ppermute | solution.py:17
  201.3 3.6 %collective-permute-done.4 = bf16[2,2,256,10,64]{2,4,3,1,0:T(8,128)(2,1)S(1)} collective-permute-done((bf16[2,2,256,10,64]{2,4,3,1,0:T(8,128)(2,1)}, bf16[2,2,256,10,64]{2,4,3,1,0:T(8,128)(2,1)S(1)}, u32[]{:S(2)}, u32[]{:S(2)}) %collective-permute-start.4) | collective-permute-done | bytes 1310752 | tf_op jit(solution)/shard_map/ppermute | solution.py:20
  211.5 7.5 %collective-permute-done.5 = bf16[2,256,640]{2,1,0:T(8,128)(2,1)S(1)} collective-permute-done((bf16[2,256,640]{2,1,0:T(8,128)(2,1)S(1)}, bf16[2,256,640]{2,1,0:T(8,128)(2,1)S(1)}, u32[]{:S(2)}, u32[]{:S(2)}) %collective-permute-start.5) | collective-permute-done | bytes 655392 | tf_op jit(solution)/shard_map/ppermute | solution.py:28
  224.4 2.5 collective-permute-start.6
  227.9 2.1 convolution_convert_fusion.2
  234.7 2.4 copy.112
  237.1 2.0 multiply_reduce_fusion.2
  239.2 15.5 %collective-permute-done.6 = bf16[2,2,256,10,64]{2,4,3,1,0:T(8,128)(2,1)S(1)} collective-permute-done((bf16[2,2,256,10,64]{2,4,3,1,0:T(8,128)(2,1)}, bf16[2,2,256,10,64]{2,4,3,1,0:T(8,128)(2,1)S(1)}, u32[]{:S(2)}, u32[]{:S(2)}) %collective-permute-start.6) | collective-permute-done | bytes 1310752 | tf_op jit(solution)/shard_map/ppermute | solution.py:17
  254.7 4.8 %collective-permute-done.7 = bf16[2,2,256,10,64]{2,4,3,1,0:T(8,128)(2,1)S(1)} collective-permute-done((bf16[2,2,256,10,64]{2,4,3,1,0:T(8,128)(2,1)}, bf16[2,2,256,10,64]{2,4,3,1,0:T(8,128)(2,1)S(1)}, u32[]{:S(2)}, u32[]{:S(2)}) %collective-permute-start.7) | collective-permute-done | bytes 1310752 | tf_op jit(solution)/shard_map/ppermute | solution.py:20
  265.8 7.5 %collective-permute-done.8 = bf16[2,256,640]{2,1,0:T(8,128)(2,1)S(1)} collective-permute-done((bf16[2,256,640]{2,1,0:T(8,128)(2,1)S(1)}, bf16[2,256,640]{2,1,0:T(8,128)(2,1)S(1)}, u32[]{:S(2)}, u32[]{:S(2)}) %collective-permute-start.8) | collective-permute-done | bytes 655392 | tf_op jit(solution)/shard_map/ppermute | solution.py:28
  (176 shorter events, 53.0 us)
Async XLA Ops:
  6.5 98.1 %copy-start = (bf16[1024,640]{1,0:T(8,128)(2,1)S(1)}, bf16[1024,640]{1,0:T(8,128)(2,1)}, u32[]{:S(2)}) copy-start(bf16[1024,640]{1,0:T(8,128)(2,1)} %param.18) | copy-start | bytes 3932164
  6.5 97.1 %all-reduce.2.cloned.1.call-start = ((), (), s32[]{:S(2)}) async-start(), calls=%async_computation | async-start | bytes 655360 | tf_op jit(solution)/shard_map/psum | solution.py:57
  11.5 93.5 %copy-start.31 = (f32[16,640]{1,0:T(8,128)S(1)}, f32[16,640]{1,0:T(8,128)}, u32[]{:S(2)}) copy-start(f32[16,640]{1,0:T(8,128)} %param.19) | copy-start | bytes 122884
  11.5 93.5 %copy-start.32 = (s32[2]{0:T(128)S(1)}, s32[2]{0:T(128)}, u32[]{:S(2)}) copy-start(s32[2]{0:T(128)} %param.14) | copy-start | bytes 28
  11.5 93.7 %copy-start.8 = (bf16[2,256,640]{2,1,0:T(8,128)(2,1)S(1)}, bf16[2,256,640]{2,1,0:T(8,128)(2,1)}, u32[]{:S(2)}) copy-start(bf16[2,256,640]{2,1,0:T(8,128)(2,1)} %param.13) | copy-start | bytes 1966084
  11.5 94.0 %copy-start.20 = (f32[640]{0:T(1024)S(1)}, f32[640]{0:T(1024)}, u32[]{:S(2)}) copy-start(f32[640]{0:T(1024)} %param.21) | copy-start | bytes 7684
  105.7 2.6 copy-start.17
  110.1 2.7 copy-start.33
  111.3 29.7 %collective-permute-start = (bf16[2,2,256,10,64]{2,4,3,1,0:T(8,128)(2,1)}, bf16[2,2,256,10,64]{2,4,3,1,0:T(8,128)(2,1)S(1)}, u32[]{:S(2)}, u32[]{:S(2)}) collective-permute-start(bf16[2,2,256,10,64]{2,4,3,1,0:T(8,128)(2,1)} %copy_dynamic-update-slice_fusion.4), channel_id=1, source_target_pairs={{0,1},{1,2},{2,3},{3,4},{4,5},{5,6},{6,7},{7,8},{8,9},{9,10},{10,1... | collective-permute-start | bytes 3932168 | tf_op jit(solution)/shard_map/ppermute | solution.py:17
  112.0 38.4 %collective-permute-start.1 = (bf16[2,2,256,10,64]{2,4,3,1,0:T(8,128)(2,1)}, bf16[2,2,256,10,64]{2,4,3,1,0:T(8,128)(2,1)S(1)}, u32[]{:S(2)}, u32[]{:S(2)}) collective-permute-start(bf16[2,2,256,10,64]{2,4,3,1,0:T(8,128)(2,1)} %copy_dynamic-update-slice_fusion.4), channel_id=1, source_target_pairs={{1,0},{2,1},{3,2},{4,3},{5,4},{6,5},{7,6},{8,7},{9,8},{10,9},{11,1... | collective-permute-start | bytes 3932168 | tf_op jit(solution)/shard_map/ppermute | solution.py:20
  123.2 27.2 %copy-start.5 = (f32[2,256,10,64]{1,0,3,2:T(2,128)S(1)}, f32[2,256,10,64]{1,0,3,2:T(2,128)}, u32[]{:S(2)}) copy-start(f32[2,256,10,64]{1,0,3,2:T(2,128)} %convert.37) | copy-start | bytes 3932164
  156.7 8.3 %copy-start.23 = (bf16[640,640]{1,0:T(8,128)(2,1)S(1)}, bf16[640,640]{1,0:T(8,128)(2,1)}, u32[]{:S(2)}) copy-start(bf16[640,640]{1,0:T(8,128)(2,1)} %param.23) | copy-start | bytes 2457604
  156.7 7.8 %collective-permute-start.2 = (bf16[2,256,640]{2,1,0:T(8,128)(2,1)S(1)}, bf16[2,256,640]{2,1,0:T(8,128)(2,1)S(1)}, u32[]{:S(2)}, u32[]{:S(2)}) collective-permute-start(bf16[2,256,640]{2,1,0:T(8,128)(2,1)S(1)} %fusion.6), channel_id=1, source_target_pairs={{15,0},{0,1},{1,2},{2,3},{3,4},{4,5},{5,6},{6,7},{7,8},{8,9},{9,10... | collective-permute-start | bytes 1966088 | tf_op jit(solution)/shard_map/ppermute | solution.py:28
  165.0 2.2 copy-start.19
  169.9 31.4 %collective-permute-start.3 = (bf16[2,2,256,10,64]{2,4,3,1,0:T(8,128)(2,1)}, bf16[2,2,256,10,64]{2,4,3,1,0:T(8,128)(2,1)S(1)}, u32[]{:S(2)}, u32[]{:S(2)}) collective-permute-start(bf16[2,2,256,10,64]{2,4,3,1,0:T(8,128)(2,1)} %copy_dynamic-update-slice_fusion.2), channel_id=1, source_target_pairs={{0,1},{1,2},{2,3},{3,4},{4,5},{5,6},{6,7},{7,8},{8,9},{9,10},{10,1... | collective-permute-start | bytes 3932168 | tf_op jit(solution)/shard_map/ppermute | solution.py:17
  172.4 32.5 %collective-permute-start.4 = (bf16[2,2,256,10,64]{2,4,3,1,0:T(8,128)(2,1)}, bf16[2,2,256,10,64]{2,4,3,1,0:T(8,128)(2,1)S(1)}, u32[]{:S(2)}, u32[]{:S(2)}) collective-permute-start(bf16[2,2,256,10,64]{2,4,3,1,0:T(8,128)(2,1)} %copy_dynamic-update-slice_fusion.2), channel_id=1, source_target_pairs={{1,0},{2,1},{3,2},{4,3},{5,4},{6,5},{7,6},{8,7},{9,8},{10,9},{11,1... | collective-permute-start | bytes 3932168 | tf_op jit(solution)/shard_map/ppermute | solution.py:20
  182.6 22.4 %copy-start.6 = (f32[2,256,10,64]{1,0,3,2:T(2,128)S(1)}, f32[2,256,10,64]{1,0,3,2:T(2,128)}, u32[]{:S(2)}) copy-start(f32[2,256,10,64]{1,0,3,2:T(2,128)} %convert.47) | copy-start | bytes 3932164
  211.2 8.3 %copy-start.24 = (bf16[640,640]{1,0:T(8,128)(2,1)S(1)}, bf16[640,640]{1,0:T(8,128)(2,1)}, u32[]{:S(2)}) copy-start(bf16[640,640]{1,0:T(8,128)(2,1)} %param.23) | copy-start | bytes 2457604
  211.2 7.8 %collective-permute-start.5 = (bf16[2,256,640]{2,1,0:T(8,128)(2,1)S(1)}, bf16[2,256,640]{2,1,0:T(8,128)(2,1)S(1)}, u32[]{:S(2)}, u32[]{:S(2)}) collective-permute-start(bf16[2,256,640]{2,1,0:T(8,128)(2,1)S(1)} %fusion.7), channel_id=1, source_target_pairs={{15,0},{0,1},{1,2},{2,3},{3,4},{4,5},{5,6},{6,7},{7,8},{8,9},{9,10... | collective-permute-start | bytes 1966088 | tf_op jit(solution)/shard_map/ppermute | solution.py:28
  224.4 30.2 %collective-permute-start.6 = (bf16[2,2,256,10,64]{2,4,3,1,0:T(8,128)(2,1)}, bf16[2,2,256,10,64]{2,4,3,1,0:T(8,128)(2,1)S(1)}, u32[]{:S(2)}, u32[]{:S(2)}) collective-permute-start(bf16[2,2,256,10,64]{2,4,3,1,0:T(8,128)(2,1)} %copy_dynamic-update-slice_fusion), channel_id=1, source_target_pairs={{0,1},{1,2},{2,3},{3,4},{4,5},{5,6},{6,7},{7,8},{8,9},{9,10},{10,1... | collective-permute-start | bytes 3932168 | tf_op jit(solution)/shard_map/ppermute | solution.py:17
  226.9 32.5 %collective-permute-start.7 = (bf16[2,2,256,10,64]{2,4,3,1,0:T(8,128)(2,1)}, bf16[2,2,256,10,64]{2,4,3,1,0:T(8,128)(2,1)S(1)}, u32[]{:S(2)}, u32[]{:S(2)}) collective-permute-start(bf16[2,2,256,10,64]{2,4,3,1,0:T(8,128)(2,1)} %copy_dynamic-update-slice_fusion), channel_id=1, source_target_pairs={{1,0},{2,1},{3,2},{4,3},{5,4},{6,5},{7,6},{8,7},{9,8},{10,9},{11,1... | collective-permute-start | bytes 3932168 | tf_op jit(solution)/shard_map/ppermute | solution.py:20
  237.1 22.4 %copy-start.7 = (f32[2,256,10,64]{1,0,3,2:T(2,128)S(1)}, f32[2,256,10,64]{1,0,3,2:T(2,128)}, u32[]{:S(2)}) copy-start(f32[2,256,10,64]{1,0,3,2:T(2,128)} %convert.57) | copy-start | bytes 3932164
  264.9 9.3 %copy-start.1 = (bf16[1024,640]{1,0:T(8,128)(2,1)S(1)}, bf16[1024,640]{1,0:T(8,128)(2,1)}, u32[]{:S(2)}) copy-start(bf16[1024,640]{1,0:T(8,128)(2,1)} %param.18) | copy-start | bytes 3932164
  265.7 7.6 %collective-permute-start.8 = (bf16[2,256,640]{2,1,0:T(8,128)(2,1)S(1)}, bf16[2,256,640]{2,1,0:T(8,128)(2,1)S(1)}, u32[]{:S(2)}, u32[]{:S(2)}) collective-permute-start(bf16[2,256,640]{2,1,0:T(8,128)(2,1)S(1)} %fusion.8), channel_id=1, source_target_pairs={{15,0},{0,1},{1,2},{2,3},{3,4},{4,5},{5,6},{6,7},{7,8},{8,9},{9,10... | collective-permute-start | bytes 1966088 | tf_op jit(solution)/shard_map/ppermute | solution.py:28
  (20 other events, 27.2 us)
Sparse Core Ops, SparseCore 0:
  11.6 91.9 all-reduce.1
where the time goes:
time: 282 us; the launch traced here: 281 us
  waiting for transfers between devices  180 us (64%)
  local copies, waits for them, and re-layouts  34.4 us (12%)
  other arithmetic  26.9 us (10%)
  matrix products  18.8 us (7%)
  between operations  14.1 us (5%)
  starting transfers between devices  6.31 us (2%)
    psum x1, waiting for transfers between devices, per_device(): pooled = jnp.mean(lax.psum(text_local, 'level'), axis=0)  92.1 us
    ppermute x3, waiting for transfers between devices, extended(): lax.ppermute(lax.slice_in_dim(block, block.shape[dim] - width, None, axis...  47.9 us
    ppermute x3, waiting for transfers between devices, shifted_2(): return lax.ppermute(block, axis, route)  22.6 us
    ppermute x3, waiting for transfers between devices, extended(): lax.ppermute(lax.slice_in_dim(block, 0, width, axis=dim), axis, backward)  17.9 us
    unnamed x18, other arithmetic  11.7 us
    dot_general x9, matrix products, project(): jnp.dot(flat, weight, preferred_element_type=jnp.float32)  10.8 us
    unnamed x72, local copies, waits for them, and re-layouts  8.87 us
    convert_element_type x3, local copies, waits for them, and re-layouts, per_device(): shifted.astype(jnp.float32)  7.16 us
  transfers between devices with their start and end apart: 10, of which 10 were waited for; matrix products, arithmetic and copies ran while one was open for 13% of the time, Pallas kernels for 0%

commit v1 on v0

--- a/solution.py
+++ b/solution.py
@@ -54,7 +54,7 @@
         text_ids[:, None] == index * vocab_rows + jnp.arange(vocab_rows, dtype=jnp.int32)[None, :]
     ).astype(jnp.bfloat16)
     text_local = jnp.dot(one_text, text_table, preferred_element_type=jnp.float32)
-    pooled = jnp.mean(lax.psum(text_local, "level"), axis=0)
+    pooled = jnp.mean(jnp.sum(lax.all_gather(text_local, "level"), axis=0), axis=0)
     text_vec = jnp.dot(
         pooled.astype(jnp.bfloat16)[None, :], text_proj, preferred_element_type=jnp.float32
     )[0]

time: 282 us -> 247 us (0.88)
  waiting for transfers between devices: 180 us -> 143 us
    psum x1 -> x0, waiting for transfers between devices: 92.1 us -> none  [per_device(): pooled = jnp.mean(lax.psum(text_local, 'level'), axis=0)]
    all_gather x0 -> x1, waiting for transfers between devices: none -> 58.4 us  [per_device(): lax.all_gather(text_local, 'level')]
    ppermute x3, waiting for transfers between devices: 17.9 us -> 13.4 us  [extended(): lax.ppermute(lax.slice_in_dim(block, 0, width, axis=dim), axis, backward)]
  transfers between devices with their start and end apart: 10 -> 10, of which waited for: 10 -> 10; matrix products, arithmetic and copies ran while one was open for 13% -> 15% of each run, Pallas kernels for 0% -> 0%
where the time goes in v1:
time: 247 us; the launch traced here: 246 us
  waiting for transfers between devices  143 us (58%)
  local copies, waits for them, and re-layouts  34.9 us (14%)
  other arithmetic  28.7 us (12%)
  matrix products  18.8 us (8%)
  between operations  14.1 us (6%)
  starting transfers between devices  6.06 us (2%)
    all_gather x1, waiting for transfers between devices, per_device(): lax.all_gather(text_local, 'level')  58.4 us
    ppermute x3, waiting for transfers between devices, extended(): lax.ppermute(lax.slice_in_dim(block, block.shape[dim] - width, None, axis...  49 us
    ppermute x3, waiting for transfers between devices, shifted_2(): return lax.ppermute(block, axis, route)  22.6 us
    ppermute x3, waiting for transfers between devices, extended(): lax.ppermute(lax.slice_in_dim(block, 0, width, axis=dim), axis, backward)  13.4 us
    unnamed x18, other arithmetic  11.7 us
    dot_general x9, matrix products, project(): jnp.dot(flat, weight, preferred_element_type=jnp.float32)  10.8 us
    unnamed x72, local copies, waits for them, and re-layouts  9.36 us
    convert_element_type x3, local copies, waits for them, and re-layouts, per_device(): shifted.astype(jnp.float32)  7.16 us
  transfers between devices with their start and end apart: 10, of which 10 were waited for; matrix products, arithmetic and copies ran while one was open for 15% of the time, Pallas kernels for 0%

profile of v1, /device:TPU:1, one launch (start us, length us, event | category | flops | bytes accessed | tf_op | source)
XLA Modules:
  0.0 245.9 jit_solution(1056351848001152587)
XLA Ops:
  6.5 4.9 %convolution_bitcast_fusion = f32[1,77,1024]{2,1,0:T(8,128)} fusion(bf16[3088,1024]{1,0:T(8,128)(2,1)} %param.17, s32[3088]{0:T(1024)S(1)} %iota_add_fusion, s32[77]{0:T(128)} %param.16), kind=kOutput, calls=%fused_computation.81 | convolution fusion | flops 487203008 | bytes 6652276 | tf_op jit(solution)/shard_map/dot_general | solution.py:56
  11.5 58.4 %all-gather.4.cloned.1.call-done = f32[16,77,1024]{2,1,0:T(8,128)} async-done(((f32[1,77,1024]{2,1,0:T(8,128)}), f32[16,77,1024]{2,1,0:T(8,128)}) %all-gather.4.cloned.1.call-update) | async-done | bytes 5046288 | tf_op jit(solution)/shard_map/all_gather | solution.py:57
  69.9 2.8 %reduce_sum.67 = f32[1024]{0:T(1024)S(1)} reduce(f32[16,77,1024]{2,1,0:T(8,128)} %all-gather.4.cloned.1.call-done, f32[]{:T(128)} %constant.8.clone.1), dimensions={0,1}, to_apply=%region_0.0 | reduce | flops 1260544 | bytes 5050372 | tf_op jit(solution)/shard_map/reduce_sum | solution.py:57
  82.3 2.1 convolution_convert_fusion.8
  85.5 2.0 reshape.375
  89.1 2.4 copy.96
  91.5 2.0 multiply_reduce_fusion.12
  93.5 15.6 %collective-permute-done = bf16[2,2,256,10,64]{2,4,3,1,0:T(8,128)(2,1)S(1)} collective-permute-done((bf16[2,2,256,10,64]{2,4,3,1,0:T(8,128)(2,1)}, bf16[2,2,256,10,64]{2,4,3,1,0:T(8,128)(2,1)S(1)}, u32[]{:S(2)}, u32[]{:S(2)}) %collective-permute-start) | collective-permute-done | bytes 1310752 | tf_op jit(solution)/shard_map/ppermute | solution.py:17
  109.2 2.4 collective-permute-done.1
  118.1 7.5 %collective-permute-done.2 = bf16[2,256,640]{2,1,0:T(8,128)(2,1)S(1)} collective-permute-done((bf16[2,256,640]{2,1,0:T(8,128)(2,1)S(1)}, bf16[2,256,640]{2,1,0:T(8,128)(2,1)S(1)}, u32[]{:S(2)}, u32[]{:S(2)}) %collective-permute-start.2) | collective-permute-done | bytes 655392 | tf_op jit(solution)/shard_map/ppermute | solution.py:28
  131.0 2.5 %collective-permute-start.3 = (bf16[2,2,256,10,64]{2,4,3,1,0:T(8,128)(2,1)}, bf16[2,2,256,10,64]{2,4,3,1,0:T(8,128)(2,1)S(1)}, u32[]{:S(2)}, u32[]{:S(2)}) collective-permute-start(bf16[2,2,256,10,64]{2,4,3,1,0:T(8,128)(2,1)} %copy_dynamic-update-slice_fusion.2), channel_id=1, source_target_pairs={{0,1},{1,2},{2,3},{3,4},{4,5},{5,6},{6,7},{7,8},{8,9},{9,10},{10,1... | collective-permute-start | bytes 3932168 | tf_op jit(solution)/shard_map/ppermute | solution.py:17
  134.5 2.1 convolution_convert_fusion.5
  141.3 2.4 copy.104
  143.7 2.0 multiply_reduce_fusion.7
  145.8 16.7 %collective-permute-done.3 = bf16[2,2,256,10,64]{2,4,3,1,0:T(8,128)(2,1)S(1)} collective-permute-done((bf16[2,2,256,10,64]{2,4,3,1,0:T(8,128)(2,1)}, bf16[2,2,256,10,64]{2,4,3,1,0:T(8,128)(2,1)S(1)}, u32[]{:S(2)}, u32[]{:S(2)}) %collective-permute-start.3) | collective-permute-done | bytes 1310752 | tf_op jit(solution)/shard_map/ppermute | solution.py:17
  162.4 7.4 %collective-permute-done.4 = bf16[2,2,256,10,64]{2,4,3,1,0:T(8,128)(2,1)S(1)} collective-permute-done((bf16[2,2,256,10,64]{2,4,3,1,0:T(8,128)(2,1)}, bf16[2,2,256,10,64]{2,4,3,1,0:T(8,128)(2,1)S(1)}, u32[]{:S(2)}, u32[]{:S(2)}) %collective-permute-start.4) | collective-permute-done | bytes 1310752 | tf_op jit(solution)/shard_map/ppermute | solution.py:20
  176.4 7.5 %collective-permute-done.5 = bf16[2,256,640]{2,1,0:T(8,128)(2,1)S(1)} collective-permute-done((bf16[2,256,640]{2,1,0:T(8,128)(2,1)S(1)}, bf16[2,256,640]{2,1,0:T(8,128)(2,1)S(1)}, u32[]{:S(2)}, u32[]{:S(2)}) %collective-permute-start.5) | collective-permute-done | bytes 655392 | tf_op jit(solution)/shard_map/ppermute | solution.py:28
  189.3 2.5 %collective-permute-start.6 = (bf16[2,2,256,10,64]{2,4,3,1,0:T(8,128)(2,1)}, bf16[2,2,256,10,64]{2,4,3,1,0:T(8,128)(2,1)S(1)}, u32[]{:S(2)}, u32[]{:S(2)}) collective-permute-start(bf16[2,2,256,10,64]{2,4,3,1,0:T(8,128)(2,1)} %copy_dynamic-update-slice_fusion), channel_id=1, source_target_pairs={{0,1},{1,2},{2,3},{3,4},{4,5},{5,6},{6,7},{7,8},{8,9},{9,10},{10,1... | collective-permute-start | bytes 3932168 | tf_op jit(solution)/shard_map/ppermute | solution.py:17
  192.8 2.1 convolution_convert_fusion.2
  199.6 2.4 copy.112
  202.0 2.0 multiply_reduce_fusion.2
  204.1 16.7 %collective-permute-done.6 = bf16[2,2,256,10,64]{2,4,3,1,0:T(8,128)(2,1)S(1)} collective-permute-done((bf16[2,2,256,10,64]{2,4,3,1,0:T(8,128)(2,1)}, bf16[2,2,256,10,64]{2,4,3,1,0:T(8,128)(2,1)S(1)}, u32[]{:S(2)}, u32[]{:S(2)}) %collective-permute-start.6) | collective-permute-done | bytes 1310752 | tf_op jit(solution)/shard_map/ppermute | solution.py:17
  220.7 3.6 %collective-permute-done.7 = bf16[2,2,256,10,64]{2,4,3,1,0:T(8,128)(2,1)S(1)} collective-permute-done((bf16[2,2,256,10,64]{2,4,3,1,0:T(8,128)(2,1)}, bf16[2,2,256,10,64]{2,4,3,1,0:T(8,128)(2,1)S(1)}, u32[]{:S(2)}, u32[]{:S(2)}) %collective-permute-start.7) | collective-permute-done | bytes 1310752 | tf_op jit(solution)/shard_map/ppermute | solution.py:20
  230.7 7.5 %collective-permute-done.8 = bf16[2,256,640]{2,1,0:T(8,128)(2,1)S(1)} collective-permute-done((bf16[2,256,640]{2,1,0:T(8,128)(2,1)S(1)}, bf16[2,256,640]{2,1,0:T(8,128)(2,1)S(1)}, u32[]{:S(2)}, u32[]{:S(2)}) %collective-permute-start.8) | collective-permute-done | bytes 655392 | tf_op jit(solution)/shard_map/ppermute | solution.py:28
  (176 shorter events, 54.2 us)
Async XLA Ops:
  6.5 66.2 %copy-start = (bf16[1024,640]{1,0:T(8,128)(2,1)S(1)}, bf16[1024,640]{1,0:T(8,128)(2,1)}, u32[]{:S(2)}) copy-start(bf16[1024,640]{1,0:T(8,128)(2,1)} %param.18) | copy-start | bytes 3932164
  6.5 63.3 %all-gather.4.cloned.1.call-start = ((), (), s32[]{:S(2)}) async-start(), calls=%async_computation | async-start | bytes 5570560 | tf_op jit(solution)/shard_map/all_gather | solution.py:57
  74.3 2.5 %copy-start.17 = (bf16[2,256,640]{2,1,0:T(8,128)(2,1)}, bf16[2,256,640]{2,1,0:T(8,128)(2,1)S(1)}, u32[]{:S(2)}) copy-start(bf16[2,256,640]{2,1,0:T(8,128)(2,1)S(1)} %fusion.17) | copy-start | bytes 1966084
  78.7 1.7 copy-start.21
  78.7 2.4 copy-start.33
  79.8 29.3 %collective-permute-start = (bf16[2,2,256,10,64]{2,4,3,1,0:T(8,128)(2,1)}, bf16[2,2,256,10,64]{2,4,3,1,0:T(8,128)(2,1)S(1)}, u32[]{:S(2)}, u32[]{:S(2)}) collective-permute-start(bf16[2,2,256,10,64]{2,4,3,1,0:T(8,128)(2,1)} %copy_dynamic-update-slice_fusion.4), channel_id=1, source_target_pairs={{0,1},{1,2},{2,3},{3,4},{4,5},{5,6},{6,7},{7,8},{8,9},{9,10},{10,1... | collective-permute-start | bytes 3932168 | tf_op jit(solution)/shard_map/ppermute | solution.py:17
  80.2 31.3 %collective-permute-start.1 = (bf16[2,2,256,10,64]{2,4,3,1,0:T(8,128)(2,1)}, bf16[2,2,256,10,64]{2,4,3,1,0:T(8,128)(2,1)S(1)}, u32[]{:S(2)}, u32[]{:S(2)}) collective-permute-start(bf16[2,2,256,10,64]{2,4,3,1,0:T(8,128)(2,1)} %copy_dynamic-update-slice_fusion.4), channel_id=1, source_target_pairs={{1,0},{2,1},{3,2},{4,3},{5,4},{6,5},{7,6},{8,7},{9,8},{10,9},{11,1... | collective-permute-start | bytes 3932168 | tf_op jit(solution)/shard_map/ppermute | solution.py:20
  91.5 20.1 %copy-start.5 = (f32[2,256,10,64]{1,0,3,2:T(2,128)S(1)}, f32[2,256,10,64]{1,0,3,2:T(2,128)}, u32[]{:S(2)}) copy-start(f32[2,256,10,64]{1,0,3,2:T(2,128)} %convert.37) | copy-start | bytes 3932164
  117.8 8.3 %copy-start.23 = (bf16[640,640]{1,0:T(8,128)(2,1)S(1)}, bf16[640,640]{1,0:T(8,128)(2,1)}, u32[]{:S(2)}) copy-start(bf16[640,640]{1,0:T(8,128)(2,1)} %param.23) | copy-start | bytes 2457604
  117.8 7.8 %collective-permute-start.2 = (bf16[2,256,640]{2,1,0:T(8,128)(2,1)S(1)}, bf16[2,256,640]{2,1,0:T(8,128)(2,1)S(1)}, u32[]{:S(2)}, u32[]{:S(2)}) collective-permute-start(bf16[2,256,640]{2,1,0:T(8,128)(2,1)S(1)} %fusion.6), channel_id=1, source_target_pairs={{15,0},{0,1},{1,2},{2,3},{3,4},{4,5},{5,6},{6,7},{7,8},{8,9},{9,10... | collective-permute-start | bytes 1966088 | tf_op jit(solution)/shard_map/ppermute | solution.py:28
  126.1 2.2 copy-start.19
  131.0 31.4 %collective-permute-start.3 = (bf16[2,2,256,10,64]{2,4,3,1,0:T(8,128)(2,1)}, bf16[2,2,256,10,64]{2,4,3,1,0:T(8,128)(2,1)S(1)}, u32[]{:S(2)}, u32[]{:S(2)}) collective-permute-start(bf16[2,2,256,10,64]{2,4,3,1,0:T(8,128)(2,1)} %copy_dynamic-update-slice_fusion.2), channel_id=1, source_target_pairs={{0,1},{1,2},{2,3},{3,4},{4,5},{5,6},{6,7},{7,8},{8,9},{9,10},{10,1... | collective-permute-start | bytes 3932168 | tf_op jit(solution)/shard_map/ppermute | solution.py:17
  133.5 36.3 %collective-permute-start.4 = (bf16[2,2,256,10,64]{2,4,3,1,0:T(8,128)(2,1)}, bf16[2,2,256,10,64]{2,4,3,1,0:T(8,128)(2,1)S(1)}, u32[]{:S(2)}, u32[]{:S(2)}) collective-permute-start(bf16[2,2,256,10,64]{2,4,3,1,0:T(8,128)(2,1)} %copy_dynamic-update-slice_fusion.2), channel_id=1, source_target_pairs={{1,0},{2,1},{3,2},{4,3},{5,4},{6,5},{7,6},{8,7},{9,8},{10,9},{11,1... | collective-permute-start | bytes 3932168 | tf_op jit(solution)/shard_map/ppermute | solution.py:20
  143.7 26.1 %copy-start.6 = (f32[2,256,10,64]{1,0,3,2:T(2,128)S(1)}, f32[2,256,10,64]{1,0,3,2:T(2,128)}, u32[]{:S(2)}) copy-start(f32[2,256,10,64]{1,0,3,2:T(2,128)} %convert.47) | copy-start | bytes 3932164
  172.4 1.5 copy-start.4
  176.1 8.3 %copy-start.24 = (bf16[640,640]{1,0:T(8,128)(2,1)S(1)}, bf16[640,640]{1,0:T(8,128)(2,1)}, u32[]{:S(2)}) copy-start(bf16[640,640]{1,0:T(8,128)(2,1)} %param.23) | copy-start | bytes 2457604
  176.1 7.8 %collective-permute-start.5 = (bf16[2,256,640]{2,1,0:T(8,128)(2,1)S(1)}, bf16[2,256,640]{2,1,0:T(8,128)(2,1)S(1)}, u32[]{:S(2)}, u32[]{:S(2)}) collective-permute-start(bf16[2,256,640]{2,1,0:T(8,128)(2,1)S(1)} %fusion.7), channel_id=1, source_target_pairs={{15,0},{0,1},{1,2},{2,3},{3,4},{4,5},{5,6},{6,7},{7,8},{8,9},{9,10... | collective-permute-start | bytes 1966088 | tf_op jit(solution)/shard_map/ppermute | solution.py:28
  184.4 2.2 copy-start.18
  189.3 31.4 %collective-permute-start.6 = (bf16[2,2,256,10,64]{2,4,3,1,0:T(8,128)(2,1)}, bf16[2,2,256,10,64]{2,4,3,1,0:T(8,128)(2,1)S(1)}, u32[]{:S(2)}, u32[]{:S(2)}) collective-permute-start(bf16[2,2,256,10,64]{2,4,3,1,0:T(8,128)(2,1)} %copy_dynamic-update-slice_fusion), channel_id=1, source_target_pairs={{0,1},{1,2},{2,3},{3,4},{4,5},{5,6},{6,7},{7,8},{8,9},{9,10},{10,1... | collective-permute-start | bytes 3932168 | tf_op jit(solution)/shard_map/ppermute | solution.py:17
  191.8 32.5 %collective-permute-start.7 = (bf16[2,2,256,10,64]{2,4,3,1,0:T(8,128)(2,1)}, bf16[2,2,256,10,64]{2,4,3,1,0:T(8,128)(2,1)S(1)}, u32[]{:S(2)}, u32[]{:S(2)}) collective-permute-start(bf16[2,2,256,10,64]{2,4,3,1,0:T(8,128)(2,1)} %copy_dynamic-update-slice_fusion), channel_id=1, source_target_pairs={{1,0},{2,1},{3,2},{4,3},{5,4},{6,5},{7,6},{8,7},{9,8},{10,9},{11,1... | collective-permute-start | bytes 3932168 | tf_op jit(solution)/shard_map/ppermute | solution.py:20
  202.0 22.4 %copy-start.7 = (f32[2,256,10,64]{1,0,3,2:T(2,128)S(1)}, f32[2,256,10,64]{1,0,3,2:T(2,128)}, u32[]{:S(2)}) copy-start(f32[2,256,10,64]{1,0,3,2:T(2,128)} %convert.57) | copy-start | bytes 3932164
  227.0 1.5 copy-start.2
  229.8 9.3 %copy-start.1 = (bf16[1024,640]{1,0:T(8,128)(2,1)S(1)}, bf16[1024,640]{1,0:T(8,128)(2,1)}, u32[]{:S(2)}) copy-start(bf16[1024,640]{1,0:T(8,128)(2,1)} %param.18) | copy-start | bytes 3932164
  230.6 7.6 %collective-permute-start.8 = (bf16[2,256,640]{2,1,0:T(8,128)(2,1)S(1)}, bf16[2,256,640]{2,1,0:T(8,128)(2,1)S(1)}, u32[]{:S(2)}, u32[]{:S(2)}) collective-permute-start(bf16[2,256,640]{2,1,0:T(8,128)(2,1)S(1)} %fusion.8), channel_id=1, source_target_pairs={{15,0},{0,1},{1,2},{2,3},{3,4},{4,5},{5,6},{6,7},{7,8},{8,9},{9,10... | collective-permute-start | bytes 1966088 | tf_op jit(solution)/shard_map/ppermute | solution.py:28
  (20 other events, 24.1 us)
Sparse Core Ops, SparseCore 0:
  11.6 58.2 all-gather.3
